TPU v7x, 128 devices: a whole 4x4x4 slice. The times are simulated.
128 devices in a mesh: dp: 4 (over y), expert: 32 (over z, x, core).
Axes of the slice: x: 4, y: 4, z: 4, core: 2. Of those that a mesh axis runs over, the one named last changes fastest.
Arguments:
- tokens: bfloat16 [16384, 4096], P(('dp', 'expert')), may hold values from -6 to 6
- cotangent: bfloat16 [16384, 4096], P(('dp', 'expert')), may hold values from -25 to 25
- routes: int32 [16384, 2], P(('dp', 'expert')), may hold values from 0 to 31, all different within a row; in each aligned block of 128 rows (0 to 127, 128 to 255, ...) at most 16 rows name the same one
- route_gates: float32 [16384, 2], P(('dp', 'expert')), may hold values from 0.2 to 1
- norm_gain: float32 [4096], replicated, may hold values from 0.25 to 1.75
- gate_matrix: bfloat16 [32, 4096, 768], P('expert'), may hold values from -0.140625 to 0.140625
- up_matrix: bfloat16 [32, 4096, 768], P('expert'), may hold values from -0.140625 to 0.140625
- down_matrix: bfloat16 [32, 4096, 768], P('expert'), may hold values from -0.21650635 to 0.21650635
Outputs:
- input_grad: bfloat16 [16384, 4096], P(('dp', 'expert'))
- gain_grad: float32 [4096], P(('dp', 'expert'))
Inputs may be any that keep to these rules, and one draw needn't show every extreme that they name: `routes`: each row names 2 different experts. In the rows of one device no expert is named more than 16 times, and in every draw some device's rows name some expert exactly 16 times.
All inputs are finite; a program needn't handle non-finite values.
Results may differ from a plain program's by a relative error of at most 0.0057.
Values may be sent and summed in bfloat16 or wider, within the bound.
A program may use at most 128 MiB of HBM per device.

v0:
```python
import jax
import jax.numpy as jnp
from jax import lax
from jax.sharding import PartitionSpec as P


def route_ranks(routes, experts):
    flat_ids = routes.reshape(-1)
    onehot = (flat_ids[:, None] == jnp.arange(experts, dtype=jnp.int32)[None, :]).astype(jnp.int32)
    before = jnp.cumsum(onehot, axis=0) - onehot
    return jnp.sum(before * onehot, axis=1).reshape(routes.shape)


def slot_positions(routes, experts, capacity):
    ranks = route_ranks(routes, experts)
    return routes * capacity + ranks


def to_owner(slot_rows, experts, capacity):
    features = slot_rows.shape[1]
    arrived = lax.all_to_all(
        slot_rows.reshape(experts, capacity, features),
        "expert",
        split_axis=0,
        concat_axis=0,
        tiled=True,
    )
    return arrived.reshape(experts * capacity, features)


def to_source(slot_rows, experts, capacity):
    features = slot_rows.shape[1]
    arrived = lax.all_to_all(
        slot_rows.reshape(experts, capacity, features),
        "expert",
        split_axis=0,
        concat_axis=0,
        tiled=True,
    )
    return arrived.reshape(experts * capacity, features)


def selectors(positions, slot_count):
    slot_ids = jnp.arange(slot_count, dtype=jnp.int32)
    return [
        (positions[:, column][:, None] == slot_ids[None, :]).astype(jnp.bfloat16)
        for column in range(positions.shape[1])
    ]


def place_rows(chosen, row_sets):
    placed = lax.dot_general(
        chosen[0], row_sets[0], (((0,), (0,)), ((), ())), preferred_element_type=jnp.float32
    )
    placed = placed + lax.dot_general(
        chosen[1], row_sets[1], (((0,), (0,)), ((), ())), preferred_element_type=jnp.float32
    )
    return placed.astype(jnp.bfloat16)


def project(expert_rows, gate_local, up_local):
    pre_gate = jnp.dot(expert_rows, gate_local, preferred_element_type=jnp.float32)
    pre_up = jnp.dot(expert_rows, up_local, preferred_element_type=jnp.float32)
    return (pre_gate, pre_up)


def shards(tokens, cotangent, routes, route_gates, norm_gain, gate_matrix, up_matrix, down_matrix):
    experts = lax.axis_size("expert")
    token_rows = tokens.shape[0]
    top_routes = routes.shape[1]
    capacity = 2 * token_rows * top_routes // experts
    slot_count = experts * capacity
    gate_local = gate_matrix[0]
    up_local = up_matrix[0]
    down_local = down_matrix[0]
    positions = slot_positions(routes, experts, capacity)
    chosen = selectors(positions, slot_count)
    outgoing = place_rows(chosen, [tokens for column in range(top_routes)])
    expert_rows = to_owner(outgoing, experts, capacity)
    pre_gate, pre_up = project(expert_rows, gate_local, up_local)
    sigmoid_gate = jax.nn.sigmoid(pre_gate)
    hidden = (pre_gate * sigmoid_gate * pre_up).astype(jnp.bfloat16)
    expert_out = lax.dot_general(
        hidden, down_local, (((1,), (1,)), ((), ())), preferred_element_type=jnp.float32
    ).astype(jnp.bfloat16)
    returned = to_source(expert_out, experts, capacity)
    combined = jnp.zeros(tokens.shape, jnp.float32)
    for column in range(top_routes):
        combined = combined + route_gates[:, column : column + 1] * jnp.dot(
            chosen[column], returned, preferred_element_type=jnp.float32
        )
    residual = tokens.astype(jnp.float32) + combined
    inverse_rms = lax.rsqrt(jnp.mean(residual * residual, axis=1, keepdims=True) + 1e-06)
    normed = residual * inverse_rms
    upstream = cotangent.astype(jnp.float32)
    gain_grad = lax.psum_scatter(
        jnp.sum(upstream * normed, axis=0), ("dp", "expert"), scatter_dimension=0, tiled=True
    )
    scaled = upstream * norm_gain[None, :]
    resid_grad = inverse_rms * (scaled - normed * jnp.mean(scaled * normed, axis=1, keepdims=True))
    weighted = [
        (route_gates[:, column : column + 1] * resid_grad).astype(jnp.bfloat16)
        for column in range(top_routes)
    ]
    route_grad = to_owner(place_rows(chosen, weighted), experts, capacity)
    hidden_grad = jnp.dot(route_grad, down_local, preferred_element_type=jnp.float32)
    gate_grad = (
        hidden_grad * pre_up * sigmoid_gate * (1.0 + pre_gate * (1.0 - sigmoid_gate))
    ).astype(jnp.bfloat16)
    up_grad = (hidden_grad * pre_gate * sigmoid_gate).astype(jnp.bfloat16)
    row_grad = lax.dot_general(
        gate_grad, gate_local, (((1,), (1,)), ((), ())), preferred_element_type=jnp.float32
    )
    row_grad = row_grad + lax.dot_general(
        up_grad, up_local, (((1,), (1,)), ((), ())), preferred_element_type=jnp.float32
    )
    back_rows = to_source(row_grad.astype(jnp.bfloat16), experts, capacity)
    moe_grad = jnp.zeros(tokens.shape, jnp.float32)
    for column in range(top_routes):
        moe_grad = moe_grad + jnp.dot(chosen[column], back_rows, preferred_element_type=jnp.float32)
    input_grad = (resid_grad + moe_grad).astype(jnp.bfloat16)
    return (input_grad, gain_grad)


def solution(mesh):
    placed = (
        P(("dp", "expert"), None),
        P(("dp", "expert"), None),
        P(("dp", "expert"), None),
        P(("dp", "expert"), None),
        P(),
        P("expert", None, None),
        P("expert", None, None),
        P("expert", None, None),
    )
    return jax.shard_map(
        shards,
        mesh=mesh,
        in_specs=placed,
        out_specs=(P(("dp", "expert"), None), P(("dp", "expert"))),
        check_vma=False,
    )
```

profile of v0, /device:TPU:1, one launch (start us, length us, event | category | flops | bytes accessed | tf_op | source)
XLA Modules:
  0.0 343.1 jit_solution(12038485837158697022)
XLA Ops:
  0.6 0.8 copy.25
  1.4 0.1 eq.59
  1.6 0.1 eq.55
  1.7 0.6 reduce-window.6
  2.3 0.2 slice_reduce_fusion
  2.5 0.1 fusion.44
  2.6 0.1 reshape.62
  2.8 0.1 copy.28
  2.8 0.7 multiply_add_fusion
  3.6 2.7 fusion.33
  6.3 0.0 copy-done.1
  6.3 0.0 slice-start.9
  6.3 1.4 add_convert_fusion.2
  7.7 0.0 slice-start.4
  7.7 60.2 %all_to_all.20 = bf16[32,16,4096]{2,1,0:T(8,128)(2,1)S(1)} all-to-all(bf16[32,16,4096]{2,1,0:T(8,128)(2,1)S(1)} %bitcast.64), channel_id=1, replica_groups=mesh['dp'=4,'expert'=32] {'expert'}, dimensions={0} | all-to-all | bytes 8388608 | tf_op jit(solution)/shard_map/all_to_all | solution.py:21
  68.0 0.0 slice-done.8
  68.0 0.0 slice-done.9
  68.0 0.0 slice-start
  68.0 3.4 fusion.10
  71.4 0.0 slice-done.4
  71.4 0.0 slice-done.5
  71.4 0.0 copy-start.5
  71.4 0.0 slice-start.1
  71.4 3.5 %fusion.6 = f32[512,768]{1,0:T(8,128)S(1)} fusion(bf16[512,4096]{1,0:T(8,128)(2,1)S(1)} %bitcast.68, bf16[1,4096,768]{2,1,0:T(8,128)(2,1)S(1)} %bitcast.75), kind=kOutput, calls=%fused_computation.9 | convolution fusion | flops 3221225472 | bytes 12058624 | tf_op jit(solution)/shard_map/dot_general | solution.py:63
  74.9 0.0 copy-done.5
  74.9 0.0 slice-done
  74.9 0.0 slice-done.1
  74.9 0.0 copy-start.8
  74.9 5.1 %fusion.12 = bf16[512,4096]{1,0:T(8,128)(2,1)} fusion(bf16[1,4096,768]{2,1,0:T(8,128)(2,1)S(1)} %bitcast.71, f32[512,768]{1,0:T(8,128)S(1)} %fusion.6, f32[512,768]{1,0:T(8,128)S(1)} %fusion.10), kind=kOutput, calls=%fused_computation.15 | convolution fusion | flops 3225681920 | bytes 13631488 | tf_op jit(solution)/shard_map/dot_general | solution.py:83
  80.0 0.0 copy-done.8
  80.0 5.0 %all-to-all-start.1 = ((bf16[32,16,4096]{2,1,0:T(8,128)(2,1)}), bf16[32,16,4096]{2,1,0:T(8,128)(2,1)}, u32[]{:S(2)}, u32[]{:S(2)}) async-start(bf16[32,16,4096]{2,1,0:T(8,128)(2,1)} %bitcast.66), calls=%async_computation.1 | async-start | bytes 8388608 | tf_op jit(solution)/shard_map/all_to_all | solution.py:33
  85.0 0.0 copy-done.4
  85.0 50.7 %all-to-all-done.1 = bf16[32,16,4096]{2,1,0:T(8,128)(2,1)} async-done(((bf16[32,16,4096]{2,1,0:T(8,128)(2,1)}), bf16[32,16,4096]{2,1,0:T(8,128)(2,1)}, u32[]{:S(2)}, u32[]{:S(2)}) %all-to-all-start.1) | async-done | bytes 4194336 | tf_op jit(solution)/shard_map/all_to_all | solution.py:33
  135.7 3.0 convolution_multiply_fusion.1
  138.7 0.0 copy-done.2
  138.7 0.0 copy-start
  138.8 0.0 copy-start.3
  138.8 3.5 %multiply_reduce_fusion = (f32[128]{0:T(128)S(1)}, f32[128,4096]{1,0:T(8,128)S(1)}) fusion(f32[128,4096]{1,0:T(8,128)S(1)} %convolution_multiply_fusion.1, bf16[512,4096]{1,0:T(8,128)(2,1)} %bitcast.10, s32[128]{0:T(128)S(1)} %get-tuple-element.6, f32[128]{0:T(128)S(1)} %get-tuple-element.4, bf16[128,4096]{1,0:T(8,128)(2,1)S(1)} %copy-done.2), kind=kOutput, calls=%fused_computation.32 | convolution fusion | flops 540082048 | bytes 9438720 | tf_op jit(solution)/shard_map/dot_general | solution.py:89
  142.2 0.0 copy-done
  142.3 0.0 copy-done.3
  142.3 0.8 fusion.25
  143.1 1.5 fusion.26
  144.6 0.0 slice-start.3
  144.6 1.6 add_convert_fusion.1
  146.2 0.0 slice-start.6
  146.2 0.0 slice-start.10
  146.3 57.7 %all_to_all.21 = bf16[32,16,4096]{2,1,0:T(8,128)(2,1)S(1)} all-to-all(bf16[32,16,4096]{2,1,0:T(8,128)(2,1)S(1)} %bitcast.63), channel_id=1, replica_groups=mesh['dp'=4,'expert'=32] {'expert'}, dimensions={0} | all-to-all | bytes 8388608 | tf_op jit(solution)/shard_map/all_to_all | solution.py:21
  203.9 0.0 slice-done.2
  203.9 0.0 slice-done.3
  203.9 0.0 copy-start.6
  203.9 0.0 slice-start.11
  203.9 3.4 fusion
  207.4 0.0 copy-start.7
  207.4 1.1 copy-done.7
  208.5 0.0 slice-done.7
  208.5 5.8 %fusion.4 = f32[512,4096]{1,0:T(8,128)} fusion(bf16[1,4096,768]{2,1,0:T(8,128)(2,1)S(1)} %bitcast.77, f32[512,768]{1,0:T(8,128)S(1)} %fusion, f32[512,768]{1,0:T(8,128)S(1)} %copy-done.6), kind=kOutput, calls=%fused_computation.7 | convolution fusion | flops 3223584768 | bytes 17825792 | tf_op jit(solution)/shard_map/dot_general | solution.py:114
  214.3 0.0 slice-done.10
  214.3 9.1 %add_convert_fusion = bf16[512,4096]{1,0:T(8,128)(2,1)} fusion(f32[512,4096]{1,0:T(8,128)} %fusion.4, bf16[1,4096,768]{2,1,0:T(8,128)(2,1)S(1)} %bitcast.81, f32[512,768]{1,0:T(8,128)S(1)} %copy-done.6, f32[512,768]{1,0:T(8,128)} %copy-done.7, f32[512,768]{1,0:T(8,128)} %copy-done.8), kind=kOutput, calls=%fused_computation | convolution fusion | flops 3229351936 | bytes 23592960 | tf_op jit(solution)/shard_map/dot_general | solution.py:111
  223.4 4.9 %all-to-all-start.3 = ((bf16[32,16,4096]{2,1,0:T(8,128)(2,1)}), bf16[32,16,4096]{2,1,0:T(8,128)(2,1)}, u32[]{:S(2)}, u32[]{:S(2)}) async-start(bf16[32,16,4096]{2,1,0:T(8,128)(2,1)} %bitcast.65), calls=%async_computation.3 | async-start | bytes 8388608 | tf_op jit(solution)/shard_map/all_to_all | solution.py:33
  228.3 106.7 %all-reduce = f32[4096]{0:T(1024)S(1)} all-reduce(f32[4096]{0:T(1024)S(1)} %get-tuple-element.2), channel_id=2, replica_groups=mesh['dp'=4,'expert'=32] {'dp','expert'}, use_global_device_ids=true, to_apply=%region_6.7.clone | all-reduce | flops 4096 | bytes 32768
  335.0 0.6 dynamic-slice
  335.6 0.0 all-to-all-done.3
  335.6 2.9 fusion.32
  338.5 4.6 %fusion.20 = bf16[128,4096]{1,0:T(8,128)(2,1)} fusion(f32[128,4096]{1,0:T(8,128)S(1)} %fusion.32, bf16[512,4096]{1,0:T(8,128)(2,1)} %bitcast.15, s32[128]{0:T(128)S(1)} %get-tuple-element.6, f32[128]{0:T(128)S(1)} %broadcast_multiply_fusion, f32[128,4096]{1,0:T(8,128)S(1)} %get-tuple-element.9, f32[4096]{0:T(1024)S(1)} %copy-done.3, ...), kind=kOutput, calls=%fused_computation.22 | convolution fusion | flops 541655040 | bytes 10503680 | tf_op jit(solution)/shard_map/dot_general | solution.py:120
  (23 shorter events, 0.1 us)
Async XLA Ops:
  3.6 2.7 copy-start.1
  3.6 64.4 %slice-start.8 = ((s8[6291456]{0:T(1024)(128)(4,1)}), s8[4194304]{0:T(1024)(128)(4,1)S(1)}, s32[]{:S(2)}) async-start(s8[6291456]{0:T(1024)(128)(4,1)} %bitcast.78), calls=%async_computation.12 | async-start | bytes 8388608
  6.3 61.6 %slice-start.9 = ((s8[6291456]{0:T(1024)(128)(4,1)}), s8[2097152]{0:T(1024)(128)(4,1)S(1)}, s32[]{:S(2)}) async-start(s8[6291456]{0:T(1024)(128)(4,1)} %bitcast.78), calls=%async_computation.13 | async-start | bytes 4194304
  7.7 63.7 %slice-start.4 = ((s8[6291456]{0:T(1024)(128)(4,1)}), s8[4194304]{0:T(1024)(128)(4,1)S(1)}, s32[]{:S(2)}) async-start(s8[6291456]{0:T(1024)(128)(4,1)} %bitcast.74), calls=%async_computation.8 | async-start | bytes 8388608
  68.0 3.4 %slice-start.5 = ((s8[6291456]{0:T(1024)(128)(4,1)}), s8[2097152]{0:T(1024)(128)(4,1)S(1)}, s32[]{:S(2)}) async-start(s8[6291456]{0:T(1024)(128)(4,1)} %bitcast.74), calls=%async_computation.9 | async-start | bytes 4194304
  68.0 6.9 %slice-start = ((s8[6291456]{0:T(1024)(128)(4,1)}), s8[4194304]{0:T(1024)(128)(4,1)S(1)}, s32[]{:S(2)}) async-start(s8[6291456]{0:T(1024)(128)(4,1)} %bitcast.70), calls=%async_computation.4 | async-start | bytes 8388608
  71.4 3.5 %copy-start.5 = (f32[512,768]{1,0:T(8,128)}, f32[512,768]{1,0:T(8,128)S(1)}, u32[]{:S(2)}) copy-start(f32[512,768]{1,0:T(8,128)S(1)} %fusion.10) | copy-start | bytes 4718596
  71.4 3.5 %slice-start.1 = ((s8[6291456]{0:T(1024)(128)(4,1)}), s8[2097152]{0:T(1024)(128)(4,1)S(1)}, s32[]{:S(2)}) async-start(s8[6291456]{0:T(1024)(128)(4,1)} %bitcast.70), calls=%async_computation.5 | async-start | bytes 4194304
  74.9 5.1 %copy-start.8 = (f32[512,768]{1,0:T(8,128)}, f32[512,768]{1,0:T(8,128)S(1)}, u32[]{:S(2)}) copy-start(f32[512,768]{1,0:T(8,128)S(1)} %fusion.6) | copy-start | bytes 4718596
  80.0 5.0 %copy-start.4 = (f32[128,2]{0,1:T(2,128)S(1)}, f32[128,2]{0,1:T(2,128)}, u32[]{:S(2)}) copy-start(f32[128,2]{0,1:T(2,128)} %param.11) | copy-start | bytes 3076
  80.0 55.7 %all-to-all-start.1 = ((bf16[32,16,4096]{2,1,0:T(8,128)(2,1)}), bf16[32,16,4096]{2,1,0:T(8,128)(2,1)}, u32[]{:S(2)}, u32[]{:S(2)}) async-start(bf16[32,16,4096]{2,1,0:T(8,128)(2,1)} %bitcast.66), calls=%async_computation.1 | async-start | bytes 8388608 | tf_op jit(solution)/shard_map/all_to_all | solution.py:33
  135.7 3.0 copy-start.2
  138.7 3.5 %copy-start = (bf16[128,4096]{1,0:T(8,128)(2,1)S(1)}, bf16[128,4096]{1,0:T(8,128)(2,1)}, u32[]{:S(2)}) copy-start(bf16[128,4096]{1,0:T(8,128)(2,1)} %param.9) | copy-start | bytes 3145732
  138.8 3.5 %copy-start.3 = (f32[4096]{0:T(1024)S(1)}, f32[4096]{0:T(1024)}, u32[]{:S(2)}) copy-start(f32[4096]{0:T(1024)} %param.12) | copy-start | bytes 49156
  143.1 60.8 %slice-start.2 = ((s8[6291456]{0:T(1024)(128)(4,1)}), s8[4194304]{0:T(1024)(128)(4,1)S(1)}, s32[]{:S(2)}) async-start(s8[6291456]{0:T(1024)(128)(4,1)} %bitcast.72), calls=%async_computation.6 | async-start | bytes 8388608
  144.6 59.3 %slice-start.3 = ((s8[6291456]{0:T(1024)(128)(4,1)}), s8[2097152]{0:T(1024)(128)(4,1)S(1)}, s32[]{:S(2)}) async-start(s8[6291456]{0:T(1024)(128)(4,1)} %bitcast.72), calls=%async_computation.7 | async-start | bytes 4194304
  146.2 62.3 %slice-start.6 = ((s8[6291456]{0:T(1024)(128)(4,1)}), s8[4194304]{0:T(1024)(128)(4,1)S(1)}, s32[]{:S(2)}) async-start(s8[6291456]{0:T(1024)(128)(4,1)} %bitcast.76), calls=%async_computation.10 | async-start | bytes 8388608
  146.2 68.1 %slice-start.10 = ((s8[6291456]{0:T(1024)(128)(4,1)}), s8[4194304]{0:T(1024)(128)(4,1)S(1)}, s32[]{:S(2)}) async-start(s8[6291456]{0:T(1024)(128)(4,1)} %bitcast.80), calls=%async_computation.14 | async-start | bytes 8388608
  203.9 4.6 %slice-start.7 = ((s8[6291456]{0:T(1024)(128)(4,1)}), s8[2097152]{0:T(1024)(128)(4,1)S(1)}, s32[]{:S(2)}) async-start(s8[6291456]{0:T(1024)(128)(4,1)} %bitcast.76), calls=%async_computation.11 | async-start | bytes 4194304
  203.9 4.6 %copy-start.6 = (f32[512,768]{1,0:T(8,128)S(1)}, f32[512,768]{1,0:T(8,128)}, u32[]{:S(2)}) copy-start(f32[512,768]{1,0:T(8,128)} %copy-done.5) | copy-start | bytes 4718596
  203.9 10.4 %slice-start.11 = ((s8[6291456]{0:T(1024)(128)(4,1)}), s8[2097152]{0:T(1024)(128)(4,1)S(1)}, s32[]{:S(2)}) async-start(s8[6291456]{0:T(1024)(128)(4,1)} %bitcast.80), calls=%async_computation.15 | async-start | bytes 4194304
  207.4 1.2 copy-start.7
  223.4 112.1 %all-to-all-start.3 = ((bf16[32,16,4096]{2,1,0:T(8,128)(2,1)}), bf16[32,16,4096]{2,1,0:T(8,128)(2,1)}, u32[]{:S(2)}, u32[]{:S(2)}) async-start(bf16[32,16,4096]{2,1,0:T(8,128)(2,1)} %bitcast.65), calls=%async_computation.3 | async-start | bytes 8388608 | tf_op jit(solution)/shard_map/all_to_all | solution.py:33
where the time goes:
time: 344 us; the launch traced here: 343 us
  blocking collectives  225 us (65%)
  matrix products  51.5 us (15%)
  waiting for transfers between devices  50.7 us (15%)
  starting transfers between devices  9.86 us (3%)
    all_to_all x2, blocking collectives, to_owner(): lax.all_to_all(slot_rows.reshape(experts, capacity, features), 'expert',...  118 us
    unnamed x1, blocking collectives  107 us
    all_to_all x2, waiting for transfers between devices, to_source(): lax.all_to_all(slot_rows.reshape(experts, capacity, features), 'expert',...  50.7 us
    all_to_all x2, starting transfers between devices, to_source(): lax.all_to_all(slot_rows.reshape(experts, capacity, features), 'expert',...  9.86 us
    dot_general x1, matrix products, shards(): lax.dot_general(gate_grad, gate_local, (((1,), (1,)), ((), ())), preferre...  9.1 us
    dot_general x2, matrix products, shards(): jnp.dot(chosen[column], back_rows, preferred_element_type=jnp.float32)  7.54 us
  transfers between devices with their start and end apart: 2, of which 1 were waited for; matrix products, arithmetic and copies ran while one was open for 0% of the time, Pallas kernels for 0%

commit v1 on v0

v1 whole, which is shorter than its diff:
```python
import functools
import jax
import jax.numpy as jnp
from jax import lax
from jax.experimental import pallas as pl
from jax.experimental.pallas import tpu as pltpu
from jax.sharding import PartitionSpec as P

MESH = pl.DeviceIdType.MESH
CHUNKS = 8
F32 = jnp.float32
BF16 = jnp.bfloat16
NT = (((1,), (1,)), ((), ()))


def peer_offsets():
    offsets = [(dz, dx, dc) for dz in range(4) for dx in range(4) for dc in range(2)][1:]
    near = lambda d: min(d, 4 - d)
    return sorted(offsets, key=lambda o: -(near(o[0]) + near(o[1])))


def dot(a, b):
    return jnp.dot(a, b, preferred_element_type=F32)


def kernel(
    dims,
    tokens, cotangent, routes, gates, gain, gate_w, up_w, down_w,
    out, gain_out,
    send_src, recv_exp, send_exp, recv_src,
    tok, cot, wg, wu, wd,
    residual, acc_a, acc_b, acc_c, half_a, half_b, place, pick, obuf,
    gsend, grecv, gsum, gall,
    load_sem, weight_sem, out_sem, send_sem, recv_sem, gain_sem,
):
    rows, features, inner, experts, cap, dps = dims
    slots = experts * cap
    width = features // CHUNKS
    me = lax.axis_index("expert")
    dp = lax.axis_index("dp")
    z, x, c = me // 8, (me // 2) % 4, me % 2
    peers = [
        ((z + dz) % 4) * 8 + ((x + dx) % 4) * 2 + (c + dc) % 2 for dz, dx, dc in peer_offsets()
    ]

    def cols(k):
        return pl.ds(pl.multiple_of(k * width, width), width)

    def block(e):
        return pl.ds(pl.multiple_of(e * cap, cap), cap)

    def tok_copy(k):
        return pltpu.make_async_copy(tokens.at[:, cols(k)], tok.at[k], load_sem.at[0, k])

    def cot_copy(k):
        return pltpu.make_async_copy(cotangent.at[:, cols(k)], cot.at[k], load_sem.at[1, k])

    def weight_copy(which, k):
        src, dst = ((gate_w, wg), (up_w, wu), (down_w, wd))[which]
        return pltpu.make_async_copy(src.at[cols(k), :], dst.at[k], weight_sem.at[which, k])

    def out_copy(k):
        return pltpu.make_async_copy(obuf.at[k], out.at[:, cols(k)], out_sem.at[k])

    barrier = pltpu.get_barrier_semaphore()
    for t in peers:
        pl.semaphore_signal(barrier, inc=1, device_id=(dp, t), device_id_type=MESH)
    for s in range(1, dps):
        pl.semaphore_signal(barrier, inc=1, device_id=((dp + s) % dps, me), device_id_type=MESH)

    for k in range(CHUNKS):
        tok_copy(k).start()
    for k in range(CHUNKS):
        weight_copy(0, k).start()
        weight_copy(1, k).start()
    for k in range(CHUNKS):
        weight_copy(2, k).start()
    for k in range(CHUNKS):
        cot_copy(k).start()

    sub = lax.broadcasted_iota(jnp.int32, (rows, rows), 0)
    lane = lax.broadcasted_iota(jnp.int32, (rows, rows), 1)
    lane_f = lane.astype(F32)
    named = routes[...].astype(F32)
    named_col = [named[:, j : j + 1] for j in range(2)]
    named_row = [
        jnp.sum(jnp.where(sub == lane, named_col[j], 0.0), axis=0, keepdims=True) for j in range(2)
    ]
    hot_col = [jnp.where(named_col[j] == lane_f, 1.0, 0.0) for j in range(2)]
    earlier = jnp.where(lane < sub, 1.0, 0.0).astype(BF16)
    before_col = dot(earlier, (hot_col[0] + hot_col[1]).astype(BF16))
    sub_f = sub.astype(F32)
    hot_row = [jnp.where(named_row[j] == sub_f, 1.0, 0.0) for j in range(2)]
    later = jnp.where(sub < lane, 1.0, 0.0).astype(BF16)
    before_row = dot((hot_row[0] + hot_row[1]).astype(BF16), later)
    slot_lane = lax.broadcasted_iota(jnp.int32, (rows, slots), 1).astype(F32)
    slot_sub = lax.broadcasted_iota(jnp.int32, (slots, rows), 0).astype(F32)
    for j in range(2):
        slot_col = named_col[j] * cap + jnp.sum(before_col * hot_col[j], axis=1, keepdims=True)
        slot_row = named_row[j] * cap + jnp.sum(before_row * hot_row[j], axis=0, keepdims=True)
        pick[pl.ds(j * rows, rows), :] = jnp.where(slot_col == slot_lane, 1.0, 0.0).astype(BF16)
        place[:, pl.ds(j * rows, rows)] = jnp.where(slot_row == slot_sub, 1.0, 0.0).astype(BF16)

    pl.semaphore_wait(barrier, experts - 1 + dps - 1)

    def send(phase, k, src, dst):
        pltpu.make_async_copy(
            src.at[k, block(me)], dst.at[k, block(me)], recv_sem.at[phase, k]
        ).start()
        for t in peers:
            pltpu.make_async_remote_copy(
                src_ref=src.at[k, block(t)],
                dst_ref=dst.at[k, block(me)],
                send_sem=send_sem.at[phase, k],
                recv_sem=recv_sem.at[phase, k],
                device_id=(dp, t),
                device_id_type=MESH,
            ).start()

    def wait_recv(phase, k, dst):
        pltpu.make_async_copy(dst.at[k], dst.at[k], recv_sem.at[phase, k]).wait()

    def wait_send(phase, k, src):
        part = src.at[k, pl.ds(0, slots - cap)]
        pltpu.make_async_copy(part, part, send_sem.at[phase, k]).wait()

    def stream(phase, make, src, dst):
        make(0)

        def step(k, carry):
            make(k)
            send(phase, k - 1, src, dst)
            return carry

        lax.fori_loop(1, CHUNKS, step, 0)
        send(phase, CHUNKS - 1, src, dst)

    both = place[:, pl.ds(0, rows)] + place[:, pl.ds(rows, rows)]

    def make_rows(k):
        tok_copy(k).wait()
        send_src[k] = dot(both, tok[k]).astype(BF16)

    stream(0, make_rows, send_src, recv_exp)

    acc_a[...] = jnp.zeros_like(acc_a)
    acc_b[...] = jnp.zeros_like(acc_b)
    acc_c[...] = jnp.zeros_like(acc_c)

    def project(k, carry):
        weight_copy(0, k).wait()
        weight_copy(1, k).wait()
        wait_recv(0, k, recv_exp)
        acc_a[...] += dot(recv_exp[k], wg[k])
        acc_b[...] += dot(recv_exp[k], wu[k])
        return carry

    lax.fori_loop(0, CHUNKS, project, 0)
    pre_gate = acc_a[...]
    half_a[...] = (pre_gate * jax.nn.sigmoid(pre_gate) * acc_b[...]).astype(BF16)

    def make_out(k):
        weight_copy(2, k).wait()
        send_exp[k] = lax.dot_general(
            half_a[...], wd[k], NT, preferred_element_type=F32
        ).astype(BF16)

    stream(1, make_out, send_exp, recv_src)

    scale = gates[...]
    scale = [scale[:, j : j + 1] for j in range(2)]

    def combine(k, carry):
        squares, products = carry
        cot_copy(k).wait()
        wait_recv(1, k, recv_src)
        taken = dot(pick[...], recv_src[k])
        row = tok[k].astype(F32) + (scale[0] * taken[:rows] + scale[1] * taken[rows:])
        residual[k] = row
        scaled = cot[k].astype(F32) * gain[:, cols(k)]
        squares = squares + jnp.sum(row * row, axis=1, keepdims=True)
        products = products + jnp.sum(scaled * row, axis=1, keepdims=True)
        return squares, products

    zero = jnp.zeros((rows, 1), F32)
    squares, products = lax.fori_loop(0, CHUNKS, combine, (zero, zero))
    inverse = lax.rsqrt(squares * (1.0 / features) + 1e-06)
    mean = products * inverse * (1.0 / features)

    per_dp = features // dps

    def make_grad(k):
        wait_send(0, k, send_src)
        normed = residual[k] * inverse
        upstream = cot[k].astype(F32)
        at = k * width
        gsend[at // per_dp, :, pl.ds(pl.multiple_of(at % per_dp, width), width)] = jnp.sum(
            upstream * normed, axis=0, keepdims=True
        )
        grad = inverse * (upstream * gain[:, cols(k)] - normed * mean)
        residual[k] = grad
        weighted = jnp.concatenate([scale[0] * grad, scale[1] * grad], axis=0).astype(BF16)
        send_src[k] = dot(place[...], weighted).astype(BF16)

    stream(2, make_grad, send_src, recv_exp)

    def gain_copy(s):
        other = (dp + s) % dps
        return pltpu.make_async_remote_copy(
            src_ref=gsend.at[other],
            dst_ref=grecv.at[dp],
            send_sem=gain_sem.at[0],
            recv_sem=gain_sem.at[1],
            device_id=(other, me),
            device_id_type=MESH,
        )

    for s in range(1, dps):
        gain_copy(s).start()
    grecv[dp] = gsend[dp]


    def take_grad(k, carry):
        wait_recv(2, k, recv_exp)
        acc_c[...] += dot(recv_exp[k], wd[k])
        return carry

    lax.fori_loop(0, CHUNKS, take_grad, 0)
    pre_gate = acc_a[...]
    sigmoid_gate = jax.nn.sigmoid(pre_gate)
    hidden_grad = acc_c[...]
    half_a[...] = (
        hidden_grad * acc_b[...] * sigmoid_gate * (1.0 + pre_gate * (1.0 - sigmoid_gate))
    ).astype(BF16)
    half_b[...] = (hidden_grad * pre_gate * sigmoid_gate).astype(BF16)

    def make_back(k):
        wait_send(1, k, send_exp)
        back = lax.dot_general(half_a[...], wg[k], NT, preferred_element_type=F32)
        back = back + lax.dot_general(half_b[...], wu[k], NT, preferred_element_type=F32)
        send_exp[k] = back.astype(BF16)

    stream(3, make_back, send_exp, recv_src)

    for s in range(1, dps):
        gain_copy(s).wait_send()
    arrived = grecv.at[pl.ds(0, dps - 1)]
    pltpu.make_async_copy(arrived, arrived, gain_sem.at[1]).wait()
    part = grecv[0]
    for s in range(1, dps):
        part = part + grecv[s]
    tiles = per_dp // 128
    each = experts // tiles
    for b in range(tiles):
        gsum[b] = part[:, b * 128 : (b + 1) * 128]

    def share_copy(t):
        return pltpu.make_async_remote_copy(
            src_ref=gsum.at[t // each],
            dst_ref=gall.at[me],
            send_sem=gain_sem.at[2],
            recv_sem=gain_sem.at[3],
            device_id=(dp, t),
            device_id_type=MESH,
        )

    for t in peers:
        share_copy(t).start()
    gall[me] = gsum[me // each]

    pair = pick[pl.ds(0, rows), :] + pick[pl.ds(rows, rows), :]

    def finish(k, carry):
        wait_recv(3, k, recv_src)
        obuf[k] = (residual[k] + dot(pair, recv_src[k])).astype(BF16)
        out_copy(k).start()
        return carry

    lax.fori_loop(0, CHUNKS, finish, 0)

    arrived = gall.at[pl.ds(0, experts - 1)]
    pltpu.make_async_copy(arrived, arrived, gain_sem.at[3]).wait()
    pltpu.make_async_copy(arrived, arrived, gain_sem.at[2]).wait()
    total = jnp.sum(gall[...], axis=0)
    lanes = 128 // each
    own = total
    for q in range(1, each):
        own = jnp.where(me % each == q, pltpu.roll(total, 128 - q * lanes, 1), own)
    gain_out[...] = own[:, :lanes]

    for k in range(CHUNKS):
        wait_send(2, k, send_src)
        wait_send(3, k, send_exp)
        out_copy(k).wait()


def shards(tokens, cotangent, routes, route_gates, norm_gain, gate_matrix, up_matrix, down_matrix):
    experts, dps = lax.axis_size("expert"), lax.axis_size("dp")
    rows, features = tokens.shape
    inner = gate_matrix.shape[2]
    cap = 2 * rows * routes.shape[1] // experts
    slots = experts * cap
    width = features // CHUNKS
    dims = (rows, features, inner, experts, cap, dps)
    anywhere = pl.BlockSpec(memory_space=pl.ANY)
    vmem = pl.BlockSpec(memory_space=pltpu.VMEM)
    dma = pltpu.SemaphoreType.DMA
    slab = lambda: pltpu.VMEM((CHUNKS, slots, width), BF16)
    weight = lambda: pltpu.VMEM((CHUNKS, width, inner), BF16)
    grads, gain_part = pl.pallas_call(
        functools.partial(kernel, dims),
        out_shape=(
            jax.ShapeDtypeStruct((rows, features), BF16),
            jax.ShapeDtypeStruct((1, features // (experts * dps)), F32),
        ),
        in_specs=[anywhere, anywhere, vmem, vmem, vmem, anywhere, anywhere, anywhere],
        out_specs=(anywhere, vmem),
        scratch_shapes=[
            slab(), slab(), slab(), slab(),
            pltpu.VMEM((CHUNKS, rows, width), BF16),
            pltpu.VMEM((CHUNKS, rows, width), BF16),
            weight(), weight(), weight(),
            pltpu.VMEM((CHUNKS, rows, width), F32),
            pltpu.VMEM((slots, inner), F32),
            pltpu.VMEM((slots, inner), F32),
            pltpu.VMEM((slots, inner), F32),
            pltpu.VMEM((slots, inner), BF16),
            pltpu.VMEM((slots, inner), BF16),
            pltpu.VMEM((slots, 2 * rows), BF16),
            pltpu.VMEM((2 * rows, slots), BF16),
            pltpu.VMEM((CHUNKS, rows, width), BF16),
            pltpu.VMEM((dps, 1, features // dps), F32),
            pltpu.VMEM((dps, 1, features // dps), F32),
            pltpu.VMEM((features // dps // 128, 1, 128), F32),
            pltpu.VMEM((experts, 1, 128), F32),
            dma((2, CHUNKS)),
            dma((3, CHUNKS)),
            dma((CHUNKS,)),
            dma((4, CHUNKS)),
            dma((4, CHUNKS)),
            dma((4,)),
        ],
        compiler_params=pltpu.CompilerParams(
            collective_id=0, has_side_effects=True, vmem_limit_bytes=63 * 2**20
        ),
        name="routed_experts",
    )(
        tokens, cotangent, routes, route_gates, norm_gain.reshape(1, features),
        gate_matrix[0], up_matrix[0], down_matrix[0],
    )
    return grads, gain_part.reshape(-1)


def solution(mesh):
    placed = (
        P(("dp", "expert"), None),
        P(("dp", "expert"), None),
        P(("dp", "expert"), None),
        P(("dp", "expert"), None),
        P(),
        P("expert", None, None),
        P("expert", None, None),
        P("expert", None, None),
    )
    return jax.shard_map(
        shards,
        mesh=mesh,
        in_specs=placed,
        out_specs=(P(("dp", "expert"), None), P(("dp", "expert"))),
        check_vma=False,
    )
```

time: 344 us -> 216 us (0.63)
  blocking collectives: 225 us -> 0 us
  Pallas kernels: 0 us -> 209 us
  matrix products: 51.5 us -> 0 us
  waiting for transfers between devices: 50.7 us -> 0 us
  starting transfers between devices: 9.86 us -> 0 us
    pallas_call x0 -> x1, Pallas kernels: none -> 209 us  [shards(): pl.pallas_call(functools.partial(kernel, dims), out_shape=(jax.ShapeDtype...]
    all_to_all x2 -> x0, blocking collectives: 118 us -> none  [to_owner(): lax.all_to_all(slot_rows.reshape(experts, capacity, features), 'expert',...]
    unnamed x1 -> x0, blocking collectives: 107 us -> none
    dot_general x14 -> x0, matrix products: 51.5 us -> none  [the longest x1 9.1 us: shards(): lax.dot_general(gate_grad, gate_local, (((1,), (1,)), ((), ())), preferre...]
    all_to_all x2 -> x0, waiting for transfers between devices: 50.7 us -> none  [to_source(): lax.all_to_all(slot_rows.reshape(experts, capacity, features), 'expert',...]
    all_to_all x2 -> x0, starting transfers between devices: 9.86 us -> none  [to_source(): lax.all_to_all(slot_rows.reshape(experts, capacity, features), 'expert',...]
    unnamed x44 -> x4, local copies, waits for them, and re-layouts: 2.63 us -> 6.29 us
  transfers between devices with their start and end apart: 2 -> 0, of which waited for: 1 -> 0; matrix products, arithmetic and copies ran while one was open for 0% -> 0% of each run, Pallas kernels for 0% -> 0%
where the time goes in v1:
time: 216 us
  Pallas kernels  209 us (97%)
  local copies, waits for them, and re-layouts  6.29 us (3%)
    pallas_call x1, Pallas kernels, shards(): pl.pallas_call(functools.partial(kernel, dims), out_shape=(jax.ShapeDtype...  209 us
    unnamed x4, local copies, waits for them, and re-layouts  6.29 us

profile of v1, /device:TPU:1, one launch (start us, length us, event | category | flops | bytes accessed | tf_op | source)
XLA Modules:
  0.0 216.1 jit_solution(13103899759910625307)
XLA Ops:
  0.6 1.4 copy.10.routes
  2.0 1.4 copy.11.gates
  3.5 209.2 %routed_experts.1 = (bf16[128,4096]{1,0:T(8,128)(2,1)}, f32[1,32]{1,0:T(1,128)}) custom-call(bf16[128,4096]{1,0:T(8,128)(2,1)} %tokens.1, bf16[128,4096]{1,0:T(8,128)(2,1)} %cotangent.1, s32[128,2]{1,0:T(8,128)} %copy.10.routes, f32[128,2]{1,0:T(8,128)} %copy.11.gates, f32[1,4096]{1,0:T(1,128)} %bitcast.8, bf16[4096,768]{1,0:T(8,128)(2,1)} %bitcast.5, ...), custom_call_target="tpu_custom_call" | custom-call | tf_op jit(solution)/shard_map/routed_experts/pallas_call | solution.py:310
  212.6 2.3 %copy.14 = bf16[128,4096]{1,0:T(8,128)(2,1)} copy(bf16[128,4096]{1,0:T(8,128)(2,1)} %get-tuple-element.8) | data formatting | bytes 2097152
  214.9 1.2 copy.15

commit v2 on v1

v2 whole, which is shorter than its diff:
```python
import functools
import jax
import jax.numpy as jnp
from jax import lax
from jax.experimental import pallas as pl
from jax.experimental.pallas import tpu as pltpu
from jax.sharding import PartitionSpec as P

MESH = pl.DeviceIdType.MESH
CHUNKS = 8
F32 = jnp.float32
BF16 = jnp.bfloat16
NT = (((1,), (1,)), ((), ()))


def peer_offsets():
    offsets = [(dz, dx, dc) for dz in range(4) for dx in range(4) for dc in range(2)][1:]
    near = lambda d: min(d, 4 - d)
    return sorted(offsets, key=lambda o: -(near(o[0]) + near(o[1])))


def dot(a, b):
    return jnp.dot(a, b, preferred_element_type=F32)


def kernel(
    dims,
    tokens, cotangent, routes, gates, gain, gate_w, up_w, down_w,
    out, gain_out,
    send_src, recv_exp, send_exp, recv_src,
    tok, cot, wg, wu, wd,
    residual, weighted, acc_a, acc_b, acc_c, half_a, half_b, place, pick, obuf,
    gsend, grecv, gsum, gall,
    load_sem, weight_sem, out_sem, send_sem, recv_sem, gain_sem,
):
    rows, features, inner, experts, cap, dps = dims
    half = experts * cap // 2
    width = features // CHUNKS
    me = lax.axis_index("expert")
    dp = lax.axis_index("dp")
    z, x, c = me // 8, (me // 2) % 4, me % 2
    groups = [
        [
            ((z + dz) % 4) * 8 + ((x + dx) % 4) * 2 + (c + dc) % 2
            for dz, dx, dc in peer_offsets()
            if dc == g
        ]
        for g in range(2)
    ]
    peers = groups[0] + groups[1]

    def cols(k):
        return pl.ds(pl.multiple_of(k * width, width), width)

    def block(e):
        return pl.ds(pl.multiple_of(e // 2 * cap, cap), cap)

    def tok_copy(k):
        return pltpu.make_async_copy(tokens.at[:, cols(k)], tok.at[k], load_sem.at[0, k])

    def cot_copy(k):
        return pltpu.make_async_copy(cotangent.at[:, cols(k)], cot.at[k], load_sem.at[1, k])

    def weight_copy(which, k):
        src, dst = ((gate_w, wg), (up_w, wu), (down_w, wd))[which]
        return pltpu.make_async_copy(src.at[cols(k), :], dst.at[k], weight_sem.at[which, k])

    def out_copy(k):
        return pltpu.make_async_copy(obuf.at[k], out.at[:, cols(k)], out_sem.at[k])

    barrier = pltpu.get_barrier_semaphore()
    for t in peers:
        pl.semaphore_signal(barrier, inc=1, device_id=(dp, t), device_id_type=MESH)
    for s in range(1, dps):
        pl.semaphore_signal(barrier, inc=1, device_id=((dp + s) % dps, me), device_id_type=MESH)

    for k in range(CHUNKS):
        tok_copy(k).start()
    for k in range(CHUNKS):
        weight_copy(0, k).start()
        weight_copy(1, k).start()
    for k in range(CHUNKS):
        weight_copy(2, k).start()
    for k in range(CHUNKS):
        cot_copy(k).start()

    sub = lax.broadcasted_iota(jnp.int32, (rows, rows), 0)
    lane = lax.broadcasted_iota(jnp.int32, (rows, rows), 1)
    lane_f, sub_f = lane.astype(F32), sub.astype(F32)

    def column(row):
        return jnp.sum(jnp.where(sub == lane, row, 0.0), axis=1, keepdims=True)

    named = routes[...].astype(F32)
    named_row = [named[j : j + 1, :] for j in range(2)]
    named_col = [column(row) for row in named_row]
    hot_col = [jnp.where(named_col[j] == lane_f, 1.0, 0.0) for j in range(2)]
    hot_row = [jnp.where(named_row[j] == sub_f, 1.0, 0.0) for j in range(2)]
    earlier = jnp.where(lane < sub, 1.0, 0.0).astype(BF16)
    later = jnp.where(sub < lane, 1.0, 0.0).astype(BF16)
    before_col = dot(earlier, (hot_col[0] + hot_col[1]).astype(BF16))
    before_row = dot((hot_row[0] + hot_row[1]).astype(BF16), later)
    core = c.astype(F32)

    def base(expert):
        chip = jnp.floor(expert * 0.5)
        return chip * cap + jnp.where(expert - 2.0 * chip == core, 0.0, float(half))

    slot_lane = lax.broadcasted_iota(jnp.int32, (rows, half), 1).astype(F32)
    slot_sub = lax.broadcasted_iota(jnp.int32, (half, rows), 0).astype(F32)
    for j in range(2):
        slot_col = base(named_col[j]) + jnp.sum(before_col * hot_col[j], axis=1, keepdims=True)
        slot_row = base(named_row[j]) + jnp.sum(before_row * hot_row[j], axis=0, keepdims=True)
        for g in range(2):
            at = pl.ds(j * rows, rows)
            pick[g, at, :] = jnp.where(slot_col - g * half == slot_lane, 1.0, 0.0).astype(BF16)
            place[g, :, at] = jnp.where(slot_row - g * half == slot_sub, 1.0, 0.0).astype(BF16)

    pl.semaphore_wait(barrier, experts - 1 + dps - 1)

    def send(phase, g, k, src, dst):
        if g == 0:
            pltpu.make_async_copy(
                src.at[g, k, block(me)], dst.at[g, k, block(me)], recv_sem.at[phase, g, k]
            ).start()
        for t in groups[g]:
            pltpu.make_async_remote_copy(
                src_ref=src.at[g, k, block(t)],
                dst_ref=dst.at[g, k, block(me)],
                send_sem=send_sem.at[phase, g, k],
                recv_sem=recv_sem.at[phase, g, k],
                device_id=(dp, t),
                device_id_type=MESH,
            ).start()

    def wait_recv(phase, g, k, dst):
        pltpu.make_async_copy(dst.at[g, k], dst.at[g, k], recv_sem.at[phase, g, k]).wait()

    def wait_send(phase, g, k, src):
        part = src.at[g, k, pl.ds(0, cap * len(groups[g]))]
        pltpu.make_async_copy(part, part, send_sem.at[phase, g, k]).wait()

    def stream(phase, g, make, src, dst):
        make(0)

        def step(k, carry):
            make(k)
            send(phase, g, k - 1, src, dst)
            return carry

        lax.fori_loop(1, CHUNKS, step, 0)
        send(phase, g, CHUNKS - 1, src, dst)

    for g in range(2):
        both = place[g, :, pl.ds(0, rows)] + place[g, :, pl.ds(rows, rows)]

        def make_rows(k):
            if g == 0:
                tok_copy(k).wait()
            send_src[g, k] = dot(both, tok[k]).astype(BF16)

        stream(0, g, make_rows, send_src, recv_exp)

    acc_a[...] = jnp.zeros_like(acc_a)
    acc_b[...] = jnp.zeros_like(acc_b)
    acc_c[...] = jnp.zeros_like(acc_c)

    for g in range(2):

        def project(k, carry):
            if g == 0:
                weight_copy(0, k).wait()
                weight_copy(1, k).wait()
            wait_recv(0, g, k, recv_exp)
            acc_a[g] += dot(recv_exp[g, k], wg[k])
            acc_b[g] += dot(recv_exp[g, k], wu[k])
            return carry

        lax.fori_loop(0, CHUNKS, project, 0)
        pre_gate = acc_a[g]
        half_a[g] = (pre_gate * jax.nn.sigmoid(pre_gate) * acc_b[g]).astype(BF16)

        def make_out(k):
            if g == 0:
                weight_copy(2, k).wait()
            send_exp[g, k] = lax.dot_general(
                half_a[g], wd[k], NT, preferred_element_type=F32
            ).astype(BF16)

        stream(1, g, make_out, send_exp, recv_src)

    scale = [column(gates[pl.ds(j, 1), :]) for j in range(2)]

    def take(g, k):
        taken = dot(pick[g], recv_src[g, k])
        return scale[0] * taken[:rows] + scale[1] * taken[rows:]

    def combine_first(k, carry):
        wait_recv(1, 0, k, recv_src)
        residual[k] = tok[k].astype(F32) + take(0, k)
        return carry

    lax.fori_loop(0, CHUNKS, combine_first, 0)

    def combine_last(k, carry):
        squares, products = carry
        cot_copy(k).wait()
        wait_recv(1, 1, k, recv_src)
        row = residual[k] + take(1, k)
        residual[k] = row
        scaled = cot[k].astype(F32) * gain[:, cols(k)]
        squares = squares + jnp.sum(row * row, axis=1, keepdims=True)
        products = products + jnp.sum(scaled * row, axis=1, keepdims=True)
        return squares, products

    zero = jnp.zeros((rows, 1), F32)
    squares, products = lax.fori_loop(0, CHUNKS, combine_last, (zero, zero))
    inverse = lax.rsqrt(squares * (1.0 / features) + 1e-06)
    mean = products * inverse * (1.0 / features)

    per_dp = features // dps
    for g in range(2):

        def make_grad(k):
            wait_send(0, g, k, send_src)
            if g == 0:
                normed = residual[k] * inverse
                upstream = cot[k].astype(F32)
                at = k * width
                gsend[at // per_dp, :, pl.ds(pl.multiple_of(at % per_dp, width), width)] = jnp.sum(
                    upstream * normed, axis=0, keepdims=True
                )
                grad = inverse * (upstream * gain[:, cols(k)] - normed * mean)
                residual[k] = grad
                for j in range(2):
                    weighted[k, pl.ds(j * rows, rows), :] = (scale[j] * grad).astype(BF16)
            send_src[g, k] = dot(place[g], weighted[k]).astype(BF16)

        stream(2, g, make_grad, send_src, recv_exp)

    def gain_copy(s):
        other = (dp + s) % dps
        return pltpu.make_async_remote_copy(
            src_ref=gsend.at[other],
            dst_ref=grecv.at[dp],
            send_sem=gain_sem.at[0],
            recv_sem=gain_sem.at[1],
            device_id=(other, me),
            device_id_type=MESH,
        )

    for s in range(1, dps):
        gain_copy(s).start()
    grecv[dp] = gsend[dp]

    for g in range(2):

        def take_grad(k, carry):
            wait_recv(2, g, k, recv_exp)
            acc_c[g] += dot(recv_exp[g, k], wd[k])
            return carry

        lax.fori_loop(0, CHUNKS, take_grad, 0)
        pre_gate = acc_a[g]
        sigmoid_gate = jax.nn.sigmoid(pre_gate)
        hidden_grad = acc_c[g]
        half_a[g] = (
            hidden_grad * acc_b[g] * sigmoid_gate * (1.0 + pre_gate * (1.0 - sigmoid_gate))
        ).astype(BF16)
        half_b[g] = (hidden_grad * pre_gate * sigmoid_gate).astype(BF16)

        def make_back(k):
            wait_send(1, g, k, send_exp)
            back = lax.dot_general(half_a[g], wg[k], NT, preferred_element_type=F32)
            back = back + lax.dot_general(half_b[g], wu[k], NT, preferred_element_type=F32)
            send_exp[g, k] = back.astype(BF16)

        stream(3, g, make_back, send_exp, recv_src)

    arrived = grecv.at[pl.ds(0, dps - 1)]
    for s in range(2):
        pltpu.make_async_copy(arrived, arrived, gain_sem.at[s]).wait()
    part = grecv[0]
    for s in range(1, dps):
        part = part + grecv[s]
    tiles = per_dp // 128
    each = experts // tiles
    for b in range(tiles):
        gsum[b] = part[:, b * 128 : (b + 1) * 128]

    for t in peers:
        pltpu.make_async_remote_copy(
            src_ref=gsum.at[t // each],
            dst_ref=gall.at[me],
            send_sem=gain_sem.at[2],
            recv_sem=gain_sem.at[3],
            device_id=(dp, t),
            device_id_type=MESH,
        ).start()
    gall[me] = gsum[me // each]

    def give(g, k):
        pair = pick[g, pl.ds(0, rows), :] + pick[g, pl.ds(rows, rows), :]
        wait_recv(3, g, k, recv_src)
        return residual[k] + dot(pair, recv_src[g, k])

    def finish_first(k, carry):
        residual[k] = give(0, k)
        return carry

    lax.fori_loop(0, CHUNKS, finish_first, 0)

    arrived = gall.at[pl.ds(0, experts - 1)]
    for s in range(2, 4):
        pltpu.make_async_copy(arrived, arrived, gain_sem.at[s]).wait()
    total = jnp.sum(gall[...], axis=0)
    lanes = 128 // each
    own = total
    for q in range(1, each):
        own = jnp.where(me % each == q, pltpu.roll(total, 128 - q * lanes, 1), own)
    gain_out[...] = own[:, :lanes]

    def finish_last(k, carry):
        obuf[k] = give(1, k).astype(BF16)
        out_copy(k).start()
        return carry

    lax.fori_loop(0, CHUNKS, finish_last, 0)

    for k in range(CHUNKS):
        for g in range(2):
            wait_send(2, g, k, send_src)
            wait_send(3, g, k, send_exp)
        out_copy(k).wait()


def shards(tokens, cotangent, routes, route_gates, norm_gain, gate_matrix, up_matrix, down_matrix):
    experts, dps = lax.axis_size("expert"), lax.axis_size("dp")
    rows, features = tokens.shape
    inner = gate_matrix.shape[2]
    cap = 2 * rows * routes.shape[1] // experts
    width = features // CHUNKS
    dims = (rows, features, inner, experts, cap, dps)
    anywhere = pl.BlockSpec(memory_space=pl.ANY)
    vmem = pl.BlockSpec(memory_space=pltpu.VMEM)
    dma = pltpu.SemaphoreType.DMA
    half = experts * cap // 2
    slab = lambda: pltpu.VMEM((2, CHUNKS, half, width), BF16)
    weight = lambda: pltpu.VMEM((CHUNKS, width, inner), BF16)
    grads, gain_part = pl.pallas_call(
        functools.partial(kernel, dims),
        out_shape=(
            jax.ShapeDtypeStruct((rows, features), BF16),
            jax.ShapeDtypeStruct((1, features // (experts * dps)), F32),
        ),
        in_specs=[anywhere, anywhere, vmem, vmem, vmem, anywhere, anywhere, anywhere],
        out_specs=(anywhere, vmem),
        scratch_shapes=[
            slab(), slab(), slab(), slab(),
            pltpu.VMEM((CHUNKS, rows, width), BF16),
            pltpu.VMEM((CHUNKS, rows, width), BF16),
            weight(), weight(), weight(),
            pltpu.VMEM((CHUNKS, rows, width), F32),
            pltpu.VMEM((CHUNKS, 2 * rows, width), BF16),
            pltpu.VMEM((2, half, inner), F32),
            pltpu.VMEM((2, half, inner), F32),
            pltpu.VMEM((2, half, inner), F32),
            pltpu.VMEM((2, half, inner), BF16),
            pltpu.VMEM((2, half, inner), BF16),
            pltpu.VMEM((2, half, 2 * rows), BF16),
            pltpu.VMEM((2, 2 * rows, half), BF16),
            pltpu.VMEM((CHUNKS, rows, width), BF16),
            pltpu.VMEM((dps, 1, features // dps), F32),
            pltpu.VMEM((dps, 1, features // dps), F32),
            pltpu.VMEM((features // dps // 128, 1, 128), F32),
            pltpu.VMEM((experts, 1, 128), F32),
            dma((2, CHUNKS)),
            dma((3, CHUNKS)),
            dma((CHUNKS,)),
            dma((4, 2, CHUNKS)),
            dma((4, 2, CHUNKS)),
            dma((4,)),
        ],
        compiler_params=pltpu.CompilerParams(
            collective_id=0, has_side_effects=True, vmem_limit_bytes=63 * 2**20
        ),
        name="routed_experts",
    )(
        tokens, cotangent, routes.T, route_gates.T, norm_gain.reshape(1, features),
        gate_matrix[0], up_matrix[0], down_matrix[0],
    )
    return grads, gain_part.reshape(-1)


def solution(mesh):
    placed = (
        P(("dp", "expert"), None),
        P(("dp", "expert"), None),
        P(("dp", "expert"), None),
        P(("dp", "expert"), None),
        P(),
        P("expert", None, None),
        P("expert", None, None),
        P("expert", None, None),
    )
    return jax.shard_map(
        shards,
        mesh=mesh,
        in_specs=placed,
        out_specs=(P(("dp", "expert"), None), P(("dp", "expert"))),
        check_vma=False,
    )
```

time: 216 us -> 205 us (0.949)
  Pallas kernels: 209 us -> 200 us
  local copies, waits for them, and re-layouts: 6.29 us -> 3.4 us
    pallas_call x1, Pallas kernels: 209 us -> 200 us  [shards(): pl.pallas_call(functools.partial(kernel, dims), out_shape=(jax.ShapeDtype...]
    unnamed x4 -> x2, local copies, waits for them, and re-layouts: 6.29 us -> 3.4 us
where the time goes in v2:
time: 205 us
  Pallas kernels  200 us (98%)
  local copies, waits for them, and re-layouts  3.4 us (2%)
    pallas_call x1, Pallas kernels, shards(): pl.pallas_call(functools.partial(kernel, dims), out_shape=(jax.ShapeDtype...  200 us

profile of v2, /device:TPU:1, one launch (start us, length us, event | category | flops | bytes accessed | tf_op | source)
XLA Modules:
  0.0 204.5 jit_solution(15364413656497284617)
XLA Ops:
  0.6 200.5 %routed_experts.1 = (bf16[128,4096]{1,0:T(8,128)(2,1)}, f32[1,32]{1,0:T(1,128)}) custom-call(bf16[128,4096]{1,0:T(8,128)(2,1)} %tokens.1, bf16[128,4096]{1,0:T(8,128)(2,1)} %cotangent.1, s32[2,128]{1,0:T(2,128)} %bitcast.11, f32[2,128]{1,0:T(2,128)} %bitcast.12, f32[1,4096]{1,0:T(1,128)} %bitcast.10, bf16[4096,768]{1,0:T(8,128)(2,1)} %bitcast.7, ...), custom_call_target="tpu_custom_call" | custom-call | tf_op jit(solution)/shard_map/routed_experts/pallas_call | solution.py:350
  201.1 2.3 %copy.12 = bf16[128,4096]{1,0:T(8,128)(2,1)} copy(bf16[128,4096]{1,0:T(8,128)(2,1)} %get-tuple-element.8) | data formatting | bytes 2097152
  203.4 1.1 copy.13

commit v3 on v2

--- a/solution.py
+++ b/solution.py
@@ -29,7 +29,7 @@
     out, gain_out,
     send_src, recv_exp, send_exp, recv_src,
     tok, cot, wg, wu, wd,
-    residual, weighted, acc_a, acc_b, acc_c, half_a, half_b, place, pick, obuf,
+    residual, acc_a, acc_b, acc_c, half_a, half_b, place, pick, obuf,
     gsend, grecv, gsum, gall,
     load_sem, weight_sem, out_sem, send_sem, recv_sem, gain_sem,
 ):
@@ -76,13 +76,6 @@
 
     for k in range(CHUNKS):
         tok_copy(k).start()
-    for k in range(CHUNKS):
-        weight_copy(0, k).start()
-        weight_copy(1, k).start()
-    for k in range(CHUNKS):
-        weight_copy(2, k).start()
-    for k in range(CHUNKS):
-        cot_copy(k).start()
 
     sub = lax.broadcasted_iota(jnp.int32, (rows, rows), 0)
     lane = lax.broadcasted_iota(jnp.int32, (rows, rows), 1)
@@ -93,12 +86,8 @@
 
     named = routes[...].astype(F32)
     named_row = [named[j : j + 1, :] for j in range(2)]
-    named_col = [column(row) for row in named_row]
-    hot_col = [jnp.where(named_col[j] == lane_f, 1.0, 0.0) for j in range(2)]
     hot_row = [jnp.where(named_row[j] == sub_f, 1.0, 0.0) for j in range(2)]
-    earlier = jnp.where(lane < sub, 1.0, 0.0).astype(BF16)
     later = jnp.where(sub < lane, 1.0, 0.0).astype(BF16)
-    before_col = dot(earlier, (hot_col[0] + hot_col[1]).astype(BF16))
     before_row = dot((hot_row[0] + hot_row[1]).astype(BF16), later)
     core = c.astype(F32)
 
@@ -106,15 +95,11 @@
         chip = jnp.floor(expert * 0.5)
         return chip * cap + jnp.where(expert - 2.0 * chip == core, 0.0, float(half))
 
-    slot_lane = lax.broadcasted_iota(jnp.int32, (rows, half), 1).astype(F32)
     slot_sub = lax.broadcasted_iota(jnp.int32, (half, rows), 0).astype(F32)
     for j in range(2):
-        slot_col = base(named_col[j]) + jnp.sum(before_col * hot_col[j], axis=1, keepdims=True)
         slot_row = base(named_row[j]) + jnp.sum(before_row * hot_row[j], axis=0, keepdims=True)
         for g in range(2):
-            at = pl.ds(j * rows, rows)
-            pick[g, at, :] = jnp.where(slot_col - g * half == slot_lane, 1.0, 0.0).astype(BF16)
-            place[g, :, at] = jnp.where(slot_row - g * half == slot_sub, 1.0, 0.0).astype(BF16)
+            place[g, :, pl.ds(j * rows, rows)] = jnp.where(slot_row - g * half == slot_sub, 1.0, 0.0).astype(BF16)
 
     pl.semaphore_wait(barrier, experts - 1 + dps - 1)
 
@@ -151,15 +136,37 @@
         lax.fori_loop(1, CHUNKS, step, 0)
         send(phase, g, CHUNKS - 1, src, dst)
 
-    for g in range(2):
-        both = place[g, :, pl.ds(0, rows)] + place[g, :, pl.ds(rows, rows)]
-
-        def make_rows(k):
-            if g == 0:
-                tok_copy(k).wait()
-            send_src[g, k] = dot(both, tok[k]).astype(BF16)
-
-        stream(0, g, make_rows, send_src, recv_exp)
+    both = [place[g, :, pl.ds(0, rows)] + place[g, :, pl.ds(rows, rows)] for g in range(2)]
+
+    def make_rows(k, carry):
+        tok_copy(k).wait()
+        for g in range(2):
+            send_src[g, k] = dot(both[g], tok[k]).astype(BF16)
+        send(0, 0, k, send_src, recv_exp)
+        weight_copy(0, k).start()
+        weight_copy(1, k).start()
+        return carry
+
+    lax.fori_loop(0, CHUNKS, make_rows, 0)
+
+    def send_rows(k, carry):
+        send(0, 1, k, send_src, recv_exp)
+        weight_copy(2, k).start()
+        cot_copy(k).start()
+        return carry
+
+    lax.fori_loop(0, CHUNKS, send_rows, 0)
+
+    named_col = [column(row) for row in named_row]
+    hot_col = [jnp.where(named_col[j] == lane_f, 1.0, 0.0) for j in range(2)]
+    earlier = jnp.where(lane < sub, 1.0, 0.0).astype(BF16)
+    before_col = dot(earlier, (hot_col[0] + hot_col[1]).astype(BF16))
+    slot_lane = lax.broadcasted_iota(jnp.int32, (rows, half), 1).astype(F32)
+    for j in range(2):
+        slot_col = base(named_col[j]) + jnp.sum(before_col * hot_col[j], axis=1, keepdims=True)
+        for g in range(2):
+            hit = slot_col - g * half == slot_lane
+            pick[g, pl.ds(j * rows, rows), :] = jnp.where(hit, 1.0, 0.0).astype(BF16)
 
     acc_a[...] = jnp.zeros_like(acc_a)
     acc_b[...] = jnp.zeros_like(acc_b)
@@ -219,24 +226,30 @@
     mean = products * inverse * (1.0 / features)
 
     per_dp = features // dps
-    for g in range(2):
-
-        def make_grad(k):
+
+    def make_grad(k, carry):
+        normed = residual[k] * inverse
+        upstream = cot[k].astype(F32)
+        at = k * width
+        gsend[at // per_dp, :, pl.ds(pl.multiple_of(at % per_dp, width), width)] = jnp.sum(
+            upstream * normed, axis=0, keepdims=True
+        )
+        grad = inverse * (upstream * gain[:, cols(k)] - normed * mean)
+        residual[k] = grad
+        rows_out = jnp.concatenate([scale[j] * grad for j in range(2)], axis=0).astype(BF16)
+        for g in range(2):
             wait_send(0, g, k, send_src)
-            if g == 0:
-                normed = residual[k] * inverse
-                upstream = cot[k].astype(F32)
-                at = k * width
-                gsend[at // per_dp, :, pl.ds(pl.multiple_of(at % per_dp, width), width)] = jnp.sum(
-                    upstream * normed, axis=0, keepdims=True
-                )
-                grad = inverse * (upstream * gain[:, cols(k)] - normed * mean)
-                residual[k] = grad
-                for j in range(2):
-                    weighted[k, pl.ds(j * rows, rows), :] = (scale[j] * grad).astype(BF16)
-            send_src[g, k] = dot(place[g], weighted[k]).astype(BF16)
-
-        stream(2, g, make_grad, send_src, recv_exp)
+            send_src[g, k] = dot(place[g], rows_out).astype(BF16)
+        send(2, 0, k, send_src, recv_exp)
+        return carry
+
+    lax.fori_loop(0, CHUNKS, make_grad, 0)
+
+    def send_grad(k, carry):
+        send(2, 1, k, send_src, recv_exp)
+        return carry
+
+    lax.fori_loop(0, CHUNKS, send_grad, 0)
 
     def gain_copy(s):
         other = (dp + s) % dps
@@ -332,6 +345,26 @@
             wait_send(2, g, k, send_src)
             wait_send(3, g, k, send_exp)
         out_copy(k).wait()
+
+
+def deliver(grads, gain_part, out, gain_out, buf, in_sem, out_sem):
+    parts = buf.shape[0]
+    rows = buf.shape[1]
+
+    def load(i):
+        return pltpu.make_async_copy(grads.at[pl.ds(i * rows, rows)], buf.at[i], in_sem.at[i])
+
+    def store(i):
+        return pltpu.make_async_copy(buf.at[i], out.at[pl.ds(i * rows, rows)], out_sem.at[i])
+
+    for i in range(parts):
+        load(i).start()
+    gain_out[...] = gain_part[...]
+    for i in range(parts):
+        load(i).wait()
+        store(i).start()
+    for i in range(parts):
+        store(i).wait()
 
 
 def shards(tokens, cotangent, routes, route_gates, norm_gain, gate_matrix, up_matrix, down_matrix):
@@ -361,7 +394,6 @@
             pltpu.VMEM((CHUNKS, rows, width), BF16),
             weight(), weight(), weight(),
             pltpu.VMEM((CHUNKS, rows, width), F32),
-            pltpu.VMEM((CHUNKS, 2 * rows, width), BF16),
             pltpu.VMEM((2, half, inner), F32),
             pltpu.VMEM((2, half, inner), F32),
             pltpu.VMEM((2, half, inner), F32),
@@ -389,6 +421,22 @@
         tokens, cotangent, routes.T, route_gates.T, norm_gain.reshape(1, features),
         gate_matrix[0], up_matrix[0], down_matrix[0],
     )
+    grads, gain_part = pl.pallas_call(
+        deliver,
+        out_shape=(
+            jax.ShapeDtypeStruct((rows, features), BF16),
+            jax.ShapeDtypeStruct(gain_part.shape, F32),
+        ),
+        in_specs=[anywhere, vmem],
+        out_specs=(anywhere, vmem),
+        scratch_shapes=[
+            pltpu.VMEM((4, rows // 4, features), BF16),
+            dma((4,)),
+            dma((4,)),
+        ],
+        compiler_params=pltpu.CompilerParams(vmem_limit_bytes=63 * 2**20),
+        name="deliver",
+    )(grads, gain_part)
     return grads, gain_part.reshape(-1)
 
 

time: 205 us -> 204 us (level)
  local copies, waits for them, and re-layouts: 3.4 us -> 0 us
  Pallas kernels: 200 us -> 203 us
    unnamed x2 -> x0, local copies, waits for them, and re-layouts: 3.4 us -> none
    pallas_call x0 -> x1, Pallas kernels: none -> 3.12 us  [shards(): pl.pallas_call(deliver, out_shape=(jax.ShapeDtypeStruct((rows, features),...]
where the time goes in v3:
time: 204 us
  Pallas kernels  203 us (100%)
    pallas_call x1, Pallas kernels, shards(): pl.pallas_call(functools.partial(kernel, dims), out_shape=(jax.ShapeDtype...  200 us

profile of v3, /device:TPU:1, one launch (start us, length us, event | category | flops | bytes accessed | tf_op | source)
XLA Modules:
  0.0 204.1 jit_solution(8889392211736970579)
XLA Ops:
  0.6 200.3 %routed_experts.1 = (bf16[128,4096]{1,0:T(8,128)(2,1)}, f32[1,32]{1,0:T(1,128)}) custom-call(bf16[128,4096]{1,0:T(8,128)(2,1)} %tokens.1, bf16[128,4096]{1,0:T(8,128)(2,1)} %cotangent.1, s32[2,128]{1,0:T(2,128)} %bitcast.11, f32[2,128]{1,0:T(2,128)} %bitcast.12, f32[1,4096]{1,0:T(1,128)} %bitcast.10, bf16[4096,768]{1,0:T(8,128)(2,1)} %bitcast.7, ...), custom_call_target="tpu_custom_call" | custom-call | tf_op jit(solution)/shard_map/routed_experts/pallas_call | solution.py:383
  201.0 3.1 %deliver.1 = (bf16[128,4096]{1,0:T(8,128)(2,1)}, f32[1,32]{1,0:T(1,128)}) custom-call(bf16[128,4096]{1,0:T(8,128)(2,1)} %get-tuple-element.6.grads, f32[1,32]{1,0:T(1,128)} %get-tuple-element.7.gain_part), custom_call_target="tpu_custom_call" | custom-call | tf_op jit(solution)/shard_map/deliver/pallas_call | solution.py:424

commit v4 on v3

--- a/solution.py
+++ b/solution.py
@@ -25,13 +25,13 @@
 
 def kernel(
     dims,
-    tokens, cotangent, routes, gates, gain, gate_w, up_w, down_w,
+    tokens, cotangent, routes_in, gates_in, gain_in, gate_w, up_w, down_w,
     out, gain_out,
     send_src, recv_exp, send_exp, recv_src,
-    tok, cot, wg, wu, wd,
-    residual, acc_a, acc_b, acc_c, half_a, half_b, place, pick, obuf,
+    tok, cot, routes, gates, gain, wg, wu, wd,
+    residual, acc_a, acc_b, acc_c, half_a, half_b, place, pick,
     gsend, grecv, gsum, gall,
-    load_sem, weight_sem, out_sem, send_sem, recv_sem, gain_sem,
+    load_sem, small_sem, weight_sem, send_sem, recv_sem, gain_sem,
 ):
     rows, features, inner, experts, cap, dps = dims
     half = experts * cap // 2
@@ -65,17 +65,23 @@
         src, dst = ((gate_w, wg), (up_w, wu), (down_w, wd))[which]
         return pltpu.make_async_copy(src.at[cols(k), :], dst.at[k], weight_sem.at[which, k])
 
-    def out_copy(k):
-        return pltpu.make_async_copy(obuf.at[k], out.at[:, cols(k)], out_sem.at[k])
-
     barrier = pltpu.get_barrier_semaphore()
     for t in peers:
         pl.semaphore_signal(barrier, inc=1, device_id=(dp, t), device_id_type=MESH)
     for s in range(1, dps):
         pl.semaphore_signal(barrier, inc=1, device_id=((dp + s) % dps, me), device_id_type=MESH)
 
+    small = [
+        pltpu.make_async_copy(src, dst, small_sem.at[i])
+        for i, (src, dst) in enumerate(((routes_in, routes), (gates_in, gates), (gain_in, gain)))
+    ]
+    for copy in small:
+        copy.start()
     for k in range(CHUNKS):
         tok_copy(k).start()
+
+    for copy in small:
+        copy.wait()
 
     sub = lax.broadcasted_iota(jnp.int32, (rows, rows), 0)
     lane = lax.broadcasted_iota(jnp.int32, (rows, rows), 1)
@@ -334,8 +340,7 @@
     gain_out[...] = own[:, :lanes]
 
     def finish_last(k, carry):
-        obuf[k] = give(1, k).astype(BF16)
-        out_copy(k).start()
+        out[:, cols(k)] = give(1, k).astype(BF16)
         return carry
 
     lax.fori_loop(0, CHUNKS, finish_last, 0)
@@ -344,27 +349,6 @@
         for g in range(2):
             wait_send(2, g, k, send_src)
             wait_send(3, g, k, send_exp)
-        out_copy(k).wait()
-
-
-def deliver(grads, gain_part, out, gain_out, buf, in_sem, out_sem):
-    parts = buf.shape[0]
-    rows = buf.shape[1]
-
-    def load(i):
-        return pltpu.make_async_copy(grads.at[pl.ds(i * rows, rows)], buf.at[i], in_sem.at[i])
-
-    def store(i):
-        return pltpu.make_async_copy(buf.at[i], out.at[pl.ds(i * rows, rows)], out_sem.at[i])
-
-    for i in range(parts):
-        load(i).start()
-    gain_out[...] = gain_part[...]
-    for i in range(parts):
-        load(i).wait()
-        store(i).start()
-    for i in range(parts):
-        store(i).wait()
 
 
 def shards(tokens, cotangent, routes, route_gates, norm_gain, gate_matrix, up_matrix, down_matrix):
@@ -374,7 +358,7 @@
     cap = 2 * rows * routes.shape[1] // experts
     width = features // CHUNKS
     dims = (rows, features, inner, experts, cap, dps)
-    anywhere = pl.BlockSpec(memory_space=pl.ANY)
+    hbm = pl.BlockSpec(memory_space=pltpu.HBM)
     vmem = pl.BlockSpec(memory_space=pltpu.VMEM)
     dma = pltpu.SemaphoreType.DMA
     half = experts * cap // 2
@@ -386,12 +370,15 @@
             jax.ShapeDtypeStruct((rows, features), BF16),
             jax.ShapeDtypeStruct((1, features // (experts * dps)), F32),
         ),
-        in_specs=[anywhere, anywhere, vmem, vmem, vmem, anywhere, anywhere, anywhere],
-        out_specs=(anywhere, vmem),
+        in_specs=[hbm] * 8,
+        out_specs=(vmem, vmem),
         scratch_shapes=[
             slab(), slab(), slab(), slab(),
             pltpu.VMEM((CHUNKS, rows, width), BF16),
             pltpu.VMEM((CHUNKS, rows, width), BF16),
+            pltpu.VMEM((2, rows), jnp.int32),
+            pltpu.VMEM((2, rows), F32),
+            pltpu.VMEM((1, features), F32),
             weight(), weight(), weight(),
             pltpu.VMEM((CHUNKS, rows, width), F32),
             pltpu.VMEM((2, half, inner), F32),
@@ -401,42 +388,30 @@
             pltpu.VMEM((2, half, inner), BF16),
             pltpu.VMEM((2, half, 2 * rows), BF16),
             pltpu.VMEM((2, 2 * rows, half), BF16),
-            pltpu.VMEM((CHUNKS, rows, width), BF16),
             pltpu.VMEM((dps, 1, features // dps), F32),
             pltpu.VMEM((dps, 1, features // dps), F32),
             pltpu.VMEM((features // dps // 128, 1, 128), F32),
             pltpu.VMEM((experts, 1, 128), F32),
             dma((2, CHUNKS)),
+            dma((3,)),
             dma((3, CHUNKS)),
-            dma((CHUNKS,)),
             dma((4, 2, CHUNKS)),
             dma((4, 2, CHUNKS)),
             dma((4,)),
         ],
         compiler_params=pltpu.CompilerParams(
-            collective_id=0, has_side_effects=True, vmem_limit_bytes=63 * 2**20
+            collective_id=0, has_side_effects=True, vmem_limit_bytes=50 * 2**20
         ),
         name="routed_experts",
     )(
-        tokens, cotangent, routes.T, route_gates.T, norm_gain.reshape(1, features),
-        gate_matrix[0], up_matrix[0], down_matrix[0],
+        *(
+            pltpu.with_memory_space_constraint(operand, pltpu.HBM)
+            for operand in (
+                tokens, cotangent, routes.T, route_gates.T, norm_gain.reshape(1, features),
+                gate_matrix[0], up_matrix[0], down_matrix[0],
+            )
+        )
     )
-    grads, gain_part = pl.pallas_call(
-        deliver,
-        out_shape=(
-            jax.ShapeDtypeStruct((rows, features), BF16),
-            jax.ShapeDtypeStruct(gain_part.shape, F32),
-        ),
-        in_specs=[anywhere, vmem],
-        out_specs=(anywhere, vmem),
-        scratch_shapes=[
-            pltpu.VMEM((4, rows // 4, features), BF16),
-            dma((4,)),
-            dma((4,)),
-        ],
-        compiler_params=pltpu.CompilerParams(vmem_limit_bytes=63 * 2**20),
-        name="deliver",
-    )(grads, gain_part)
     return grads, gain_part.reshape(-1)
 
 

time: 204 us -> 201 us (0.985)
  Pallas kernels: 203 us -> 199 us
    pallas_call x1 -> x0, Pallas kernels: 3.12 us -> none  [shards(): pl.pallas_call(deliver, out_shape=(jax.ShapeDtypeStruct((rows, features),...]
where the time goes in v4:
time: 201 us
  Pallas kernels  199 us (99%)
    pallas_call x1, Pallas kernels, shards(): pl.pallas_call(functools.partial(kernel, dims), out_shape=(jax.ShapeDtype...  199 us

profile of v4, /device:TPU:1, one launch (start us, length us, event | category | flops | bytes accessed | tf_op | source)
XLA Modules:
  0.0 200.7 jit_solution(14800688408096517607)
XLA Ops:
  0.6 198.6 %routed_experts.1 = (bf16[128,4096]{1,0:T(8,128)(2,1)S(1)}, f32[1,32]{1,0:T(1,128)S(1)}) custom-call(bf16[128,4096]{1,0:T(8,128)(2,1)} %tokens.1, bf16[128,4096]{1,0:T(8,128)(2,1)} %cotangent.1, s32[2,128]{1,0:T(2,128)} %bitcast.12, f32[2,128]{1,0:T(2,128)} %bitcast.13, f32[1,4096]{1,0:T(1,128)} %bitcast.11, bf16[4096,768]{1,0:T(8,128)(2,1)} %bitcast.8, ...), custom_call_target="tpu_custom_call" | custom-call | tf_op jit(solution)/shard_map/routed_experts/pallas_call | solution.py:367
  199.2 1.0 copy.12
  200.2 0.5 copy.13

commit v5 on v4

--- a/solution.py
+++ b/solution.py
@@ -29,9 +29,10 @@
     out, gain_out,
     send_src, recv_exp, send_exp, recv_src,
     tok, cot, routes, gates, gain, wg, wu, wd,
-    residual, acc_a, acc_b, acc_c, half_a, half_b, place, pick,
+    residual, grads, far, far_routes, far_gates, acc_a, acc_b, acc_c, half_a, half_b,
+    place, slot_gate, pick,
     gsend, grecv, gsum, gall,
-    load_sem, small_sem, weight_sem, send_sem, recv_sem, gain_sem,
+    load_sem, small_sem, weight_sem, send_sem, recv_sem, line_send, line_recv, table_sem, gain_sem,
 ):
     rows, features, inner, experts, cap, dps = dims
     half = experts * cap // 2
@@ -80,32 +81,42 @@
     for k in range(CHUNKS):
         tok_copy(k).start()
 
-    for copy in small:
-        copy.wait()
-
     sub = lax.broadcasted_iota(jnp.int32, (rows, rows), 0)
     lane = lax.broadcasted_iota(jnp.int32, (rows, rows), 1)
     lane_f, sub_f = lane.astype(F32), sub.astype(F32)
+    later = jnp.where(sub < lane, 1.0, 0.0).astype(BF16)
+    z_f, x_f, c_f = z.astype(F32), x.astype(F32), c.astype(F32)
 
     def column(row):
         return jnp.sum(jnp.where(sub == lane, row, 0.0), axis=1, keepdims=True)
 
-    named = routes[...].astype(F32)
-    named_row = [named[j : j + 1, :] for j in range(2)]
-    hot_row = [jnp.where(named_row[j] == sub_f, 1.0, 0.0) for j in range(2)]
-    later = jnp.where(sub < lane, 1.0, 0.0).astype(BF16)
-    before_row = dot((hot_row[0] + hot_row[1]).astype(BF16), later)
-    core = c.astype(F32)
-
-    def base(expert):
-        chip = jnp.floor(expert * 0.5)
-        return chip * cap + jnp.where(expert - 2.0 * chip == core, 0.0, float(half))
-
-    slot_sub = lax.broadcasted_iota(jnp.int32, (half, rows), 0).astype(F32)
-    for j in range(2):
-        slot_row = base(named_row[j]) + jnp.sum(before_row * hot_row[j], axis=0, keepdims=True)
-        for g in range(2):
-            place[g, :, pl.ds(j * rows, rows)] = jnp.where(slot_row - g * half == slot_sub, 1.0, 0.0).astype(BF16)
+    def rows_of(ref):
+        values = ref[...].astype(F32)
+        return [values[j : j + 1, :] for j in range(2)]
+
+    def fill_place(named, scales, lines, p):
+        hot = [jnp.where(row == sub_f, 1.0, 0.0) for row in named]
+        before = dot((hot[0] + hot[1]).astype(BF16), later)
+        hits = {line: [] for line in lines}
+        for j in range(2):
+            rank = jnp.sum(before * hot[j], axis=0, keepdims=True)
+            chip = jnp.floor(named[j] * 0.5)
+            far_core = jnp.where(named[j] - 2.0 * chip == c_f, 0.0, 64.0)
+            z_e = jnp.floor(chip * 0.25)
+            x_e = chip - 4.0 * z_e
+            for line in lines:
+                mine, place_on = ((z_e == z_f, x_e), (x_e == x_f, z_e))[line]
+                slot = jnp.where(mine, far_core + place_on * cap + rank, -1.0)
+                hits[line].append(jnp.where(slot == sub_f, 1.0, 0.0))
+        for line in lines:
+            place[line, p] = (hits[line][0] + hits[line][1]).astype(BF16)
+            weight = jnp.sum(
+                hits[line][0] * scales[0] + hits[line][1] * scales[1], axis=1, keepdims=True
+            )
+            slot_gate[line, p] = jnp.broadcast_to(weight, (rows, rows))
+
+    for copy in small:
+        copy.wait()
 
     pl.semaphore_wait(barrier, experts - 1 + dps - 1)
 
@@ -142,26 +153,161 @@
         lax.fori_loop(1, CHUNKS, step, 0)
         send(phase, g, CHUNKS - 1, src, dst)
 
-    both = [place[g, :, pl.ds(0, rows)] + place[g, :, pl.ds(rows, rows)] for g in range(2)]
-
-    def make_rows(k, carry):
-        tok_copy(k).wait()
-        for g in range(2):
-            send_src[g, k] = dot(both[g], tok[k]).astype(BF16)
-        send(0, 0, k, send_src, recv_exp)
+    def device(zz, xx, cc):
+        return zz % 4 * 8 + xx % 4 * 2 + cc
+
+    def on_line(line, p):
+        return device(z + p, x, c) if line == 0 else device(z, x + p, c)
+
+    def across(line, q, g):
+        cc = (c + g) % 2
+        return device(z, x + q, cc) if line == 0 else device(z + q, x, cc)
+
+    def line_copy(step, k, line, d, src, dst, send, recv):
+        return pltpu.make_async_remote_copy(
+            src_ref=src,
+            dst_ref=dst,
+            send_sem=line_send.at[step, send],
+            recv_sem=line_recv.at[step, k, recv],
+            device_id=(dp, on_line(line, d)),
+            device_id_type=MESH,
+        )
+
+    def start_line(step, k, line, held):
+        for d in (1, 3):
+            line_copy(step, k, line, d, held.at[k], far.at[k, 3 - d], 0, 3 - d).start()
+
+    def wait_line(step, k, p):
+        part = far.at[k, p - 1]
+        pltpu.make_async_copy(part, part, line_recv.at[step, k, p - 1]).wait()
+
+    def relay(step, k, line):
+        for p, at in ((3, 0), (1, rows // 2)):
+            wait_line(step, k, p)
+            part = pl.ds(at, rows // 2)
+            line_copy(
+                step, k, line, 4 - p, far.at[k, p - 1, part], far.at[k, 1, part], 1, 1
+            ).start()
+
+    def wait_line_sends(step):
+        for end in range(2):
+            part = far.at[:, pl.ds(0, 2 - end)]
+            pltpu.make_async_copy(part, part, line_send.at[step, end]).wait()
+
+    def send_named(phase, g, k, line):
+        for p in (0, 3, 1, 2):
+            source = block(on_line(line, p))
+            for q in range(4):
+                axis = (x, z)[line]
+                start = p * 4 * cap + (axis + q) % 4 * cap
+                part = send_src.at[g, k, pl.ds(pl.multiple_of(start, cap), cap)]
+                arrive = recv_exp.at[g, k, source]
+                if g == 0 and q == 0:
+                    pltpu.make_async_copy(part, arrive, recv_sem.at[phase, g, k]).start()
+                else:
+                    pltpu.make_async_remote_copy(
+                        src_ref=part,
+                        dst_ref=arrive,
+                        send_sem=send_sem.at[phase, g, k],
+                        recv_sem=recv_sem.at[phase, g, k],
+                        device_id=(dp, across(line, q, g)),
+                        device_id_type=MESH,
+                    ).start()
+
+    def wait_named(phase, g, k):
+        part = send_src.at[g, k, pl.ds(0, cap * (12 + 4 * g))]
+        pltpu.make_async_copy(part, part, send_sem.at[phase, g, k]).wait()
+
+    def dispatch(phase, step, held):
+        for line in range(2):
+            relay(step, line, line)
+
+        def choose(pair, carry):
+            @pl.when(pair + 1 < CHUNKS // 2)
+            def _():
+                for line in range(2):
+                    relay(step, 2 * pair + 2 + line, line)
+
+            for line in range(2):
+                k = 2 * pair + line
+                if step == 1:
+                    for g in range(2):
+                        wait_named(0, g, k)
+                for p in (0, 3, 1, 2):
+                    if p == 2:
+                        wait_line(step, k, 2)
+                    source = held[k] if p == 0 else far[k, p - 1]
+                    chosen = dot(place[line, p], source)
+                    if step == 1:
+                        chosen = chosen * slot_gate[line, p][:, :1]
+                    chosen = chosen.astype(BF16)
+                    for g in range(2):
+                        send_src[g, k, pl.ds(p * 4 * cap, 4 * cap), :] = chosen[
+                            g * 4 * cap : (g + 1) * 4 * cap
+                        ]
+                send_named(phase, 0, k, line)
+            return carry
+
+        lax.fori_loop(0, CHUNKS // 2, choose, 0)
+
+        def send_rest(pair, carry):
+            for line in range(2):
+                send_named(phase, 1, 2 * pair + line, line)
+            return carry
+
+        lax.fori_loop(0, CHUNKS // 2, send_rest, 0)
+
+    def table_copies(line, p):
+        return [
+            pltpu.make_async_remote_copy(
+                src_ref=src,
+                dst_ref=dst.at[line, 3 - p],
+                send_sem=table_sem.at[i, 0],
+                recv_sem=table_sem.at[i, 1],
+                device_id=(dp, on_line(line, p)),
+                device_id_type=MESH,
+            )
+            for i, (src, dst) in enumerate(((routes, far_routes), (gates, far_gates)))
+        ]
+
+    for line in range(2):
+        for p in range(1, 4):
+            for copy in table_copies(line, p):
+                copy.start()
+
+    def start_tokens(pair, carry):
+        for line in range(2):
+            k = 2 * pair + line
+            tok_copy(k).wait()
+            start_line(0, k, line, tok)
+        return carry
+
+    lax.fori_loop(0, CHUNKS // 2, start_tokens, 0)
+    for k in range(CHUNKS):
         weight_copy(0, k).start()
         weight_copy(1, k).start()
-        return carry
-
-    lax.fori_loop(0, CHUNKS, make_rows, 0)
-
-    def send_rows(k, carry):
-        send(0, 1, k, send_src, recv_exp)
+    for k in range(CHUNKS):
         weight_copy(2, k).start()
         cot_copy(k).start()
-        return carry
-
-    lax.fori_loop(0, CHUNKS, send_rows, 0)
+
+    named_row = rows_of(routes)
+    fill_place(named_row, rows_of(gates), (0, 1), 0)
+    for i, table in enumerate((far_routes, far_gates)):
+        for end in range(2):
+            pltpu.make_async_copy(table, table, table_sem.at[i, end]).wait()
+    for line in range(2):
+        for p in range(1, 4):
+            fill_place(
+                rows_of(far_routes.at[line, p - 1]), rows_of(far_gates.at[line, p - 1]), (line,), p
+            )
+    dispatch(0, 0, tok)
+    wait_line_sends(0)
+
+    core = c.astype(F32)
+
+    def base(expert):
+        chip = jnp.floor(expert * 0.5)
+        return chip * cap + jnp.where(expert - 2.0 * chip == core, 0.0, float(half))
 
     named_col = [column(row) for row in named_row]
     hot_col = [jnp.where(named_col[j] == lane_f, 1.0, 0.0) for j in range(2)]
@@ -233,29 +379,24 @@
 
     per_dp = features // dps
 
-    def make_grad(k, carry):
-        normed = residual[k] * inverse
-        upstream = cot[k].astype(F32)
-        at = k * width
-        gsend[at // per_dp, :, pl.ds(pl.multiple_of(at % per_dp, width), width)] = jnp.sum(
-            upstream * normed, axis=0, keepdims=True
-        )
-        grad = inverse * (upstream * gain[:, cols(k)] - normed * mean)
-        residual[k] = grad
-        rows_out = jnp.concatenate([scale[j] * grad for j in range(2)], axis=0).astype(BF16)
-        for g in range(2):
-            wait_send(0, g, k, send_src)
-            send_src[g, k] = dot(place[g], rows_out).astype(BF16)
-        send(2, 0, k, send_src, recv_exp)
+    def make_grad(pair, carry):
+        for line in range(2):
+            k = 2 * pair + line
+            normed = residual[k] * inverse
+            grad = inverse * (cot[k].astype(F32) * gain[:, cols(k)] - normed * mean)
+            grads[k] = grad.astype(BF16)
+            at = k * width
+            gsend[at // per_dp, :, pl.ds(pl.multiple_of(at % per_dp, width), width)] = jnp.sum(
+                cot[k].astype(F32) * normed, axis=0, keepdims=True
+            )
+            residual[k] = grad
+            if line == 1:
+                start_line(1, k - 1, 0, grads)
+        start_line(1, 2 * pair + 1, 1, grads)
         return carry
 
-    lax.fori_loop(0, CHUNKS, make_grad, 0)
-
-    def send_grad(k, carry):
-        send(2, 1, k, send_src, recv_exp)
-        return carry
-
-    lax.fori_loop(0, CHUNKS, send_grad, 0)
+    lax.fori_loop(0, CHUNKS // 2, make_grad, 0)
+    dispatch(2, 1, grads)
 
     def gain_copy(s):
         other = (dp + s) % dps
@@ -347,8 +488,9 @@
 
     for k in range(CHUNKS):
         for g in range(2):
-            wait_send(2, g, k, send_src)
+            wait_named(2, g, k)
             wait_send(3, g, k, send_exp)
+    wait_line_sends(1)
 
 
 def shards(tokens, cotangent, routes, route_gates, norm_gain, gate_matrix, up_matrix, down_matrix):
@@ -381,12 +523,17 @@
             pltpu.VMEM((1, features), F32),
             weight(), weight(), weight(),
             pltpu.VMEM((CHUNKS, rows, width), F32),
+            pltpu.VMEM((CHUNKS, rows, width), BF16),
+            pltpu.VMEM((CHUNKS, 3, rows, width), BF16),
+            pltpu.VMEM((2, 3, 2, rows), jnp.int32),
+            pltpu.VMEM((2, 3, 2, rows), F32),
             pltpu.VMEM((2, half, inner), F32),
             pltpu.VMEM((2, half, inner), F32),
             pltpu.VMEM((2, half, inner), F32),
             pltpu.VMEM((2, half, inner), BF16),
             pltpu.VMEM((2, half, inner), BF16),
-            pltpu.VMEM((2, half, 2 * rows), BF16),
+            pltpu.VMEM((2, 4, rows, rows), BF16),
+            pltpu.VMEM((2, 4, rows, rows), F32),
             pltpu.VMEM((2, 2 * rows, half), BF16),
             pltpu.VMEM((dps, 1, features // dps), F32),
             pltpu.VMEM((dps, 1, features // dps), F32),
@@ -397,10 +544,13 @@
             dma((3, CHUNKS)),
             dma((4, 2, CHUNKS)),
             dma((4, 2, CHUNKS)),
+            dma((2, 2)),
+            dma((2, CHUNKS, 3)),
+            dma((2, 2)),
             dma((4,)),
         ],
         compiler_params=pltpu.CompilerParams(
-            collective_id=0, has_side_effects=True, vmem_limit_bytes=50 * 2**20
+            collective_id=0, has_side_effects=True, vmem_limit_bytes=52 * 2**20
         ),
         name="routed_experts",
     )(

time: 201 us -> 190 us (0.945)
  Pallas kernels: 199 us -> 188 us
    pallas_call x1, Pallas kernels: 199 us -> 188 us  [shards(): pl.pallas_call(functools.partial(kernel, dims), out_shape=(jax.ShapeDtype...]
where the time goes in v5:
time: 190 us
  Pallas kernels  188 us (99%)
    pallas_call x1, Pallas kernels, shards(): pl.pallas_call(functools.partial(kernel, dims), out_shape=(jax.ShapeDtype...  188 us

profile of v5, /device:TPU:1, one launch (start us, length us, event | category | flops | bytes accessed | tf_op | source)
XLA Modules:
  0.0 190.4 jit_solution(7825121706839425656)
XLA Ops:
  0.6 188.2 %routed_experts.1 = (bf16[128,4096]{1,0:T(8,128)(2,1)S(1)}, f32[1,32]{1,0:T(1,128)S(1)}) custom-call(bf16[128,4096]{1,0:T(8,128)(2,1)} %tokens.1, bf16[128,4096]{1,0:T(8,128)(2,1)} %cotangent.1, s32[2,128]{1,0:T(2,128)} %bitcast.12, f32[2,128]{1,0:T(2,128)} %bitcast.13, f32[1,4096]{1,0:T(1,128)} %bitcast.11, bf16[4096,768]{1,0:T(8,128)(2,1)} %bitcast.8, ...), custom_call_target="tpu_custom_call" | custom-call | tf_op jit(solution)/shard_map/routed_experts/pallas_call | solution.py:509
  188.9 1.0 copy.12
  189.8 0.5 copy.13

commit v6 on v5

--- a/solution.py
+++ b/solution.py
@@ -219,14 +219,14 @@
         pltpu.make_async_copy(part, part, send_sem.at[phase, g, k]).wait()
 
     def dispatch(phase, step, held):
-        for line in range(2):
-            relay(step, line, line)
+        for k in range(4):
+            relay(step, k, k % 2)
 
         def choose(pair, carry):
-            @pl.when(pair + 1 < CHUNKS // 2)
+            @pl.when(pair + 2 < CHUNKS // 2)
             def _():
                 for line in range(2):
-                    relay(step, 2 * pair + 2 + line, line)
+                    relay(step, 2 * pair + 4 + line, line)
 
             for line in range(2):
                 k = 2 * pair + line

time: 190 us -> 190 us (level)
  no operation moved by 1% of the time
where the time goes in v6:
time: 190 us; the launch traced here: 189 us
  Pallas kernels  187 us (98%)
    pallas_call x1, Pallas kernels, shards(): pl.pallas_call(functools.partial(kernel, dims), out_shape=(jax.ShapeDtype...  187 us

profile of v6, /device:TPU:1, one launch (start us, length us, event | category | flops | bytes accessed | tf_op | source)
XLA Modules:
  0.0 189.4 jit_solution(17786457378821512985)
XLA Ops:
  0.6 187.3 %routed_experts.1 = (bf16[128,4096]{1,0:T(8,128)(2,1)S(1)}, f32[1,32]{1,0:T(1,128)S(1)}) custom-call(bf16[128,4096]{1,0:T(8,128)(2,1)} %tokens.1, bf16[128,4096]{1,0:T(8,128)(2,1)} %cotangent.1, s32[2,128]{1,0:T(2,128)} %bitcast.12, f32[2,128]{1,0:T(2,128)} %bitcast.13, f32[1,4096]{1,0:T(1,128)} %bitcast.11, bf16[4096,768]{1,0:T(8,128)(2,1)} %bitcast.8, ...), custom_call_target="tpu_custom_call" | custom-call | tf_op jit(solution)/shard_map/routed_experts/pallas_call | solution.py:509
  187.9 1.0 copy.12
  188.9 0.5 copy.13
